TPU v7x, 32 devices: a whole 2x2x4 slice. The times are simulated.
32 devices in a mesh: dp: 2 (over core), row: 4 (over z), col: 4 (over y, x).
Axes of the slice: x: 2, y: 2, z: 4, core: 2. Of those that a mesh axis runs over, the one named last changes fastest.
Arguments:
- inputs: bfloat16 [512, 12288], P('dp', 'col'), may hold values from -6 to 6
- weight_tiles: bfloat16 [4, 4, 432, 4096], P('row', 'col', 'dp'), may hold values from -0.109375 to 0.109375
- tile_rows: int32 [4, 4, 432], P('row', 'col'), may hold values from 0 to 191, as said below
- tile_cols: int32 [4, 4, 432], P('row', 'col'), may hold values from 0 to 47, as said below
- tile_counts: int32 [4, 4], P('row', 'col'), may hold values from 54 to 432, as said below
- act_grad: bfloat16 [512, 49152], P('dp', ('row', 'col')), may hold values from -6 to 6
Outputs:
- activation: bfloat16 [512, 49152], P('dp', ('row', 'col'))
- input_grad: bfloat16 [512, 12288], P(('dp', 'row'), 'col')
- tile_grads: bfloat16 [4, 4, 432, 4096], P('row', 'col', 'dp')
Inputs may be any that keep to these rules, and one draw needn't show every extreme that they name: `tile_rows`: block row of a slot within its region; within each region the slots name distinct blocks. `tile_cols`: block column of a slot within its region. `tile_counts`: live slots of a region are its first ones; some region has all 432 slots live.
All inputs are finite; a program needn't handle non-finite values.
Results may differ from a plain program's by a relative error of at most 0.015.
Values may be sent and summed in bfloat16 or wider, within the bound.
No kernel may reach another device: no remote copies, remote signals or barrier semaphores. Data moves between devices by JAX's collectives and lax.ppermute only.
A program may use at most 128 MiB of HBM per device.

v0:
```python
import jax
import jax.numpy as jnp
from jax import lax
from jax.sharding import PartitionSpec as P

COEFF = 0.7978845608028654
CUBIC = 0.044715


def gelu_value(values):
    return 0.5 * values * (1.0 + jnp.tanh(COEFF * (values + CUBIC * values * values * values)))


def gelu_slope(values):
    inner = jnp.tanh(COEFF * (values + CUBIC * values * values * values))
    return 0.5 * (1.0 + inner) + 0.5 * values * (1.0 - inner * inner) * COEFF * (
        1.0 + 3.0 * CUBIC * values * values
    )


def group_loop(slot_count, advance, initial, widest):
    group_width = max((divisor for divisor in range(1, widest + 1) if slot_count % divisor == 0))

    def looped(group_index, running):
        return advance(running, group_index * group_width, group_width)

    return lax.fori_loop(0, slot_count // group_width, looped, initial)


def one_hot_rows(block_ids, block_total):
    return (block_ids[:, None] == jnp.arange(block_total)[None, :]).astype(jnp.bfloat16)


def pick_blocks(table, block_ids):
    selector = one_hot_rows(block_ids, table.shape[0])
    flat = table.reshape(table.shape[0], table.shape[1] * table.shape[2])
    picked = jnp.dot(selector, flat, preferred_element_type=jnp.float32).astype(jnp.bfloat16)
    return picked.reshape(block_ids.shape[0], table.shape[1], table.shape[2])


def place_blocks(running, products, block_ids):
    selector = one_hot_rows(block_ids, running.shape[0])
    flat = products.reshape(products.shape[0], products.shape[1] * products.shape[2])
    upper = flat.astype(jnp.bfloat16)
    lower = (flat - upper.astype(jnp.float32)).astype(jnp.bfloat16)
    added = jnp.dot(selector.T, upper, preferred_element_type=jnp.float32)
    added = added + jnp.dot(selector.T, lower, preferred_element_type=jnp.float32)
    return running + added.reshape(running.shape)


def local(inputs, weight_tiles, tile_rows, tile_cols, tile_counts, act_grad):
    token_count = inputs.shape[0]
    in_blocks = inputs.shape[1] // 64
    col_devices = lax.axis_size("col")
    share = act_grad.shape[1]
    out_blocks = share * col_devices // 64
    max_slots = tile_rows.shape[2]
    row_ids = tile_rows.reshape(max_slots)
    col_ids = tile_cols.reshape(max_slots)
    alive = (jnp.arange(max_slots) < tile_counts.reshape(())).astype(jnp.float32)
    input_blocks = inputs.T.reshape(in_blocks, 64, token_count)

    def slot_info(slot_start, group_width):
        rows_here = lax.dynamic_slice_in_dim(row_ids, slot_start, group_width)
        cols_here = lax.dynamic_slice_in_dim(col_ids, slot_start, group_width)
        alive_here = lax.dynamic_slice_in_dim(alive, slot_start, group_width)
        return (rows_here, cols_here, alive_here)

    empty_rows = jnp.zeros((out_blocks, 64, token_count), jnp.float32)
    piece = lax.all_gather(weight_tiles, "dp", axis=2, tiled=True)
    start = jnp.int32(0)
    piece_slots = piece.shape[2]
    piece_tiles = piece.reshape(piece_slots, 64, 64)

    def advance(inner_total, first, group_width):
        group_tiles = lax.dynamic_slice_in_dim(piece_tiles, first, group_width, 0)
        rows_here, cols_here, alive_here = slot_info(start + first, group_width)
        gathered = pick_blocks(input_blocks, cols_here)
        products = jnp.einsum(
            "sik,skt->sit", group_tiles, gathered, preferred_element_type=jnp.float32
        )
        products = products * alive_here[:, None, None]
        return place_blocks(inner_total, products, rows_here)

    pre_partial = group_loop(piece_slots, advance, empty_rows, 144)
    pre_partial = pre_partial.reshape(out_blocks * 64, token_count)
    pre_share = (
        lax.psum_scatter(pre_partial.astype(jnp.bfloat16), "col", scatter_dimension=0, tiled=True)
        .astype(jnp.float32)
        .T
    )
    activation = gelu_value(pre_share).astype(jnp.bfloat16)
    grad_share = (act_grad.astype(jnp.float32) * gelu_slope(pre_share)).astype(jnp.bfloat16)
    grad_full = lax.all_gather(grad_share, "col", axis=1, tiled=True)
    grad_blocks = grad_full.T.reshape(out_blocks, 64, token_count)
    empty_cols = jnp.zeros((in_blocks, 64, token_count), jnp.float32)
    piece = lax.all_gather(weight_tiles, "dp", axis=2, tiled=True)
    backward_start = jnp.int32(0)
    piece_slots = piece.shape[2]
    backward_piece_tiles = piece.reshape(piece_slots, 64, 64)

    def advance(inner_total, first, group_width):
        group_tiles = lax.dynamic_slice_in_dim(backward_piece_tiles, first, group_width, 0)
        rows_here, cols_here, alive_here = slot_info(backward_start + first, group_width)
        gathered = pick_blocks(grad_blocks, rows_here)
        products = jnp.einsum(
            "sik,sit->skt", group_tiles, gathered, preferred_element_type=jnp.float32
        )
        products = products * alive_here[:, None, None]
        return place_blocks(inner_total, products, cols_here)

    input_partial = group_loop(piece_slots, advance, empty_cols, 144)
    input_partial = input_partial.reshape(in_blocks * 64, token_count)
    input_grad = (
        lax.psum_scatter(input_partial.astype(jnp.bfloat16), "row", scatter_dimension=1, tiled=True)
        .astype(jnp.float32)
        .T.astype(jnp.bfloat16)
    )
    stored_slots = max_slots // lax.axis_size("dp")

    def advance(buffer, first, group_width):
        rows_here, cols_here, alive_here = slot_info(first, group_width)
        grads_here = pick_blocks(grad_blocks, rows_here)
        inputs_here = pick_blocks(input_blocks, cols_here)
        products = jnp.einsum(
            "sit,skt->sik", grads_here, inputs_here, preferred_element_type=jnp.float32
        )
        products = (products * alive_here[:, None, None]).reshape(group_width, 4096)
        return lax.dynamic_update_slice_in_dim(buffer, products, first, 0)

    tile_sum = lax.psum_scatter(
        group_loop(
            lax.axis_size("dp") * stored_slots,
            advance,
            jnp.zeros((lax.axis_size("dp") * stored_slots, 4096), jnp.float32),
            48,
        ).astype(jnp.bfloat16),
        "dp",
        scatter_dimension=0,
        tiled=True,
    )
    tile_grads = tile_sum.reshape(1, 1, stored_slots, 4096)
    return (activation, input_grad, tile_grads)


def solution(mesh):
    return jax.shard_map(
        local,
        mesh=mesh,
        in_specs=(
            P("dp", "col"),
            P("row", "col", "dp", None),
            P("row", "col", None),
            P("row", "col", None),
            P("row", "col"),
            P("dp", ("row", "col")),
        ),
        out_specs=(P("dp", ("row", "col")), P(("dp", "row"), "col"), P("row", "col", "dp", None)),
        check_vma=False,
    )
```

profile of v0, /device:TPU:0, one launch (start us, length us, event | category | flops | bytes accessed | tf_op | source)
XLA Modules:
  0.0 620.6 jit_solution(8441548578228094327)
XLA Ops:
  11.2 13.8 %all-gather.3.cloned.1.call-done = bf16[1,1,432,4096]{3,2,1,0:T(8,128)(2,1)} async-done(((bf16[1,1,216,4096]{3,2,1,0:T(8,128)(2,1)}), bf16[1,1,432,4096]{3,2,1,0:T(8,128)(2,1)}) %all-gather.3.cloned.1.call-update) | async-done | bytes 3538960 | tf_op jit(solution)/shard_map/all_gather | solution.py:70
  25.0 6.4 %copy.22 = bf16[1,1,432,4096]{2,3,1,0:T(8,128)(2,1)} copy(bf16[1,1,432,4096]{3,2,1,0:T(8,128)(2,1)} %all-gather.3.cloned.1.call-done) | data formatting | bytes 7077888 | tf_op jit(solution)/shard_map/all_gather | solution.py:70
  31.4 220.8 %while.45 = (s32[]{:T(128)}, f32[192,64,256]{2,1,0:T(8,128)}, s32[432]{0:T(512)S(1)}, bf16[432,64,64]{0,2,1:T(8,128)(2,1)}, s32[432]{0:T(512)S(1)}, /*index=5*/b...) while((s32[]{:T(128)}, f32[192,64,256]{2,1,0:T(8,128)}, ...), condition=%wide.wide.region_1.0_spmd.clone, body=%wide.wide.region_0.0_spmd.clone.sunk | while | flops 2366436096 | bytes 200939408 | solution.py:27
  33.0 3.5 copy.65
  39.0 3.8 copy.64
  42.9 3.7 broadcast_multiply_fusion.6
  46.6 11.4 %copy.66 = f32[18,8,64,256]{3,1,2,0:T(8,128)} copy(f32[18,8,64,256]{3,2,1,0:T(8,128)S(1)} %bitcast.144) | data formatting | bytes 18874368 | tf_op jit(solution)/shard_map/while
  58.0 5.6 fusion.72
  63.6 13.7 %convolution_add_fusion.6 = f32[192,16384]{1,0:T(8,128)} fusion(f32[192,16384]{1,0:T(8,128)S(1)} %fusion.72, f32[144,16384]{1,0:T(8,128)} %bitcast.142, s32[144]{0:T(256)S(1)} %dynamic_slice.115), kind=kOutput, calls=%fused_computation.8.clone.clone.1 | convolution fusion | flops 918580224 | bytes 34603584 | tf_op jit(solution)/shard_map/while/body/eval_jaxpr/dot_general | solution.py:47
  77.4 13.8 %copy.67 = f32[24,8,64,256]{3,2,1,0:T(8,128)} copy(f32[24,8,64,256]{3,1,2,0:T(8,128)} %bitcast.143) | data formatting | bytes 25165824 | tf_op jit(solution)/shard_map/while
  91.2 11.8 %bitcast_add_fusion.6 = f32[192,64,256]{2,1,0:T(8,128)} fusion(f32[24,8,64,256]{3,2,1,0:T(8,128)} %copy.67, f32[192,64,256]{2,1,0:T(8,128)} %get-tuple-element.774, pred[]{:T(512)S(6)} %compare.8), kind=kLoop, calls=%fused_computation.10.clone.clone.1 | loop fusion | flops 6291456 | bytes 37748736 | tf_op jit(solution)/shard_map/while/body/eval_jaxpr/add | solution.py:48
  104.5 3.5 copy.65
  108.1 2.5 constant_dynamic-slice_fusion.6
  110.5 3.8 copy.64
  114.4 3.7 broadcast_multiply_fusion.6
  118.1 11.4 %copy.66 = f32[18,8,64,256]{3,1,2,0:T(8,128)} copy(f32[18,8,64,256]{3,2,1,0:T(8,128)S(1)} %bitcast.144) | data formatting | bytes 18874368 | tf_op jit(solution)/shard_map/while
  129.6 5.6 fusion.72
  135.2 13.7 %convolution_add_fusion.6 = f32[192,16384]{1,0:T(8,128)} fusion(f32[192,16384]{1,0:T(8,128)S(1)} %fusion.72, f32[144,16384]{1,0:T(8,128)} %bitcast.142, s32[144]{0:T(256)S(1)} %dynamic_slice.115), kind=kOutput, calls=%fused_computation.8.clone.clone.1 | convolution fusion | flops 918580224 | bytes 34603584 | tf_op jit(solution)/shard_map/while/body/eval_jaxpr/dot_general | solution.py:47
  148.9 13.8 %copy.67 = f32[24,8,64,256]{3,2,1,0:T(8,128)} copy(f32[24,8,64,256]{3,1,2,0:T(8,128)} %bitcast.143) | data formatting | bytes 25165824 | tf_op jit(solution)/shard_map/while
  162.8 14.7 %bitcast_add_fusion.6 = f32[192,64,256]{2,1,0:T(8,128)} fusion(f32[24,8,64,256]{3,2,1,0:T(8,128)} %copy.67, f32[192,64,256]{2,1,0:T(8,128)} %get-tuple-element.774, pred[]{:T(512)S(6)} %compare.8), kind=kLoop, calls=%fused_computation.10.clone.clone.1 | loop fusion | flops 6291456 | bytes 37748736 | tf_op jit(solution)/shard_map/while/body/eval_jaxpr/add | solution.py:48
  179.0 3.5 copy.65
  185.0 3.8 copy.64
  188.8 3.7 broadcast_multiply_fusion.6
  192.6 11.4 %copy.66 = f32[18,8,64,256]{3,1,2,0:T(8,128)} copy(f32[18,8,64,256]{3,2,1,0:T(8,128)S(1)} %bitcast.144) | data formatting | bytes 18874368 | tf_op jit(solution)/shard_map/while
  204.0 5.6 fusion.72
  209.6 13.7 %convolution_add_fusion.6 = f32[192,16384]{1,0:T(8,128)} fusion(f32[192,16384]{1,0:T(8,128)S(1)} %fusion.72, f32[144,16384]{1,0:T(8,128)} %bitcast.142, s32[144]{0:T(256)S(1)} %dynamic_slice.115), kind=kOutput, calls=%fused_computation.8.clone.clone.1 | convolution fusion | flops 918580224 | bytes 34603584 | tf_op jit(solution)/shard_map/while/body/eval_jaxpr/dot_general | solution.py:47
  223.3 13.8 %copy.67 = f32[24,8,64,256]{3,2,1,0:T(8,128)} copy(f32[24,8,64,256]{3,1,2,0:T(8,128)} %bitcast.143) | data formatting | bytes 25165824 | tf_op jit(solution)/shard_map/while
  237.2 14.7 %bitcast_add_fusion.6 = f32[192,64,256]{2,1,0:T(8,128)} fusion(f32[24,8,64,256]{3,2,1,0:T(8,128)} %copy.67, f32[192,64,256]{2,1,0:T(8,128)} %get-tuple-element.774, pred[]{:T(512)S(6)} %compare.8), kind=kLoop, calls=%fused_computation.10.clone.clone.1 | loop fusion | flops 6291456 | bytes 37748736 | tf_op jit(solution)/shard_map/while/body/eval_jaxpr/add | solution.py:48
  252.2 8.2 %convert_element_type.122 = bf16[192,64,256]{2,1,0:T(8,128)(2,1)} convert(f32[192,64,256]{2,1,0:T(8,128)} %get-tuple-element.375) | non-fusion elementwise | flops 3145728 | bytes 18874368 | tf_op jit(solution)/shard_map/convert_element_type | solution.py:88
  262.6 69.4 %reduce-scatter.6.cloned.1.call-done = bf16[3072,256]{1,0:T(8,128)(2,1)} async-done(((bf16[12288,256]{1,0:T(8,128)(2,1)}), bf16[3072,256]{1,0:T(8,128)(2,1)}) %reduce-scatter.6.cloned.1.call-update) | async-done | bytes 1572880 | tf_op jit(solution)/shard_map/reduce_scatter | solution.py:88
  332.0 4.7 fusion.20
  338.9 68.1 %all-gather.5.cloned.1.call-done = bf16[256,12288]{0,1:T(8,128)(2,1)} async-done(((bf16[256,3072]{0,1:T(8,128)(2,1)}), bf16[256,12288]{0,1:T(8,128)(2,1)}) %all-gather.5.cloned.1.call-update) | async-done | bytes 6291472 | tf_op jit(solution)/shard_map/all_gather | solution.py:94
  407.0 10.5 %reshape_reshape.30 = bf16[192,16384]{1,0:T(8,128)(2,1)} reshape(bf16[12288,256]{1,0:T(8,128)(2,1)} %bitcast.156) | data formatting | bytes 12582912 | tf_op jit(solution)/shard_map/while/body/eval_jaxpr/reshape;reshape | solution.py:36
  417.5 10.4 %reshape_reshape.36 = bf16[192,16384]{1,0:T(8,128)(2,1)} reshape(bf16[12288,256]{1,0:T(8,128)(2,1)} %bitcast.157) | data formatting | bytes 12582912 | tf_op jit(solution)/shard_map/while/body/eval_jaxpr/reshape;reshape | solution.py:36
  427.9 98.9 %while.46 = (s32[]{:T(128)}, f32[48,64,256]{2,1,0:T(8,128)}, s32[432]{0:T(512)S(1)}, bf16[432,64,64]{0,2,1:T(8,128)(2,1)}, s32[432]{0:T(512)S(1)}, /*index=5*/bf...) while((s32[]{:T(128)}, f32[48,64,256]{2,1,0:T(8,128)}, ...), condition=%wide.wide.region_4.0_spmd.clone, body=%wide.wide.region_3.0_spmd.clone.sunk | while | flops 1679860224 | bytes 117577552 | solution.py:27
  428.2 4.2 convolution_convert_fusion.15
  432.4 3.6 copy.69
  437.1 4.5 copy.68
  441.7 4.4 broadcast_multiply_fusion.7
  446.1 7.7 %copy.70 = f32[18,8,64,256]{3,1,2,0:T(8,128)S(1)} copy(f32[18,8,64,256]{3,2,1,0:T(8,128)S(1)} %bitcast.145) | data formatting | bytes 18874368 | tf_op jit(solution)/shard_map/while
  457.2 2.5 bitcast_add_fusion.7
  459.8 4.2 convolution_convert_fusion.15
  464.0 3.6 copy.69
  468.7 4.5 copy.68
  473.3 4.4 broadcast_multiply_fusion.7
  477.8 7.7 %copy.70 = f32[18,8,64,256]{3,1,2,0:T(8,128)S(1)} copy(f32[18,8,64,256]{3,2,1,0:T(8,128)S(1)} %bitcast.145) | data formatting | bytes 18874368 | tf_op jit(solution)/shard_map/while
  488.8 4.4 bitcast_add_fusion.7
  493.3 4.2 convolution_convert_fusion.15
  497.5 3.6 copy.69
  502.2 4.5 copy.68
  506.8 4.4 broadcast_multiply_fusion.7
  511.2 7.7 %copy.70 = f32[18,8,64,256]{3,1,2,0:T(8,128)S(1)} copy(f32[18,8,64,256]{3,2,1,0:T(8,128)S(1)} %bitcast.145) | data formatting | bytes 18874368 | tf_op jit(solution)/shard_map/while
  522.2 4.4 bitcast_add_fusion.7
  533.0 69.1 %while.44 = (s32[]{:T(128)}, bf16[432,4096]{1,0:T(8,128)(2,1)}, s32[432]{0:T(512)S(1)}, bf16[12288,256]{1,0:T(8,128)(2,1)}, s32[432]{0:T(512)S(1)}, /*index=5*/b...) while((s32[]{:T(128)}, bf16[432,4096]{1,0:T(8,128)(2,1)}, ...), condition=%wide.wide.region_7.0_spmd, body=%wide.wide.region_6.0_spmd.sunk | while | flops 480128256 | bytes 22415228 | solution.py:27
  533.0 4.1 convolution_convert_fusion.12
  540.7 4.1 convolution_convert_fusion.12
  548.4 4.1 convolution_convert_fusion.12
  556.1 4.1 convolution_convert_fusion.12
  563.8 4.1 convolution_convert_fusion.12
  571.5 4.1 convolution_convert_fusion.12
  579.1 4.1 convolution_convert_fusion.12
  586.8 4.1 convolution_convert_fusion.12
  594.5 4.1 convolution_convert_fusion.12
  605.3 8.5 %reduce-scatter.8.cloned.1.call-done = bf16[216,4096]{1,0:T(8,128)(2,1)} async-done(((bf16[432,4096]{1,0:T(8,128)(2,1)}), bf16[216,4096]{1,0:T(8,128)(2,1)}) %reduce-scatter.8.cloned.1.call-update) | async-done | bytes 1769488 | tf_op jit(solution)/shard_map/reduce_scatter | solution.py:131
  (176 shorter events, 72.2 us)
Async XLA Ops:
  7.2 17.8 %all-gather.3.cloned.1.call-start = ((), (), s32[]{:S(2)}) async-start(), calls=%async_computation.3 | async-start | bytes 5308416 | tf_op jit(solution)/shard_map/all_gather | solution.py:70
  7.9 324.1 %reduce-scatter.6.cloned.1.call-start = ((), (), s32[]{:S(2)}) async-start(), calls=%async_computation.4 | async-start | bytes 7864320 | tf_op jit(solution)/shard_map/reduce_scatter | solution.py:88
  9.7 21.7 %copy-start.5 = (bf16[256,3072]{0,1:T(8,128)(2,1)}, bf16[256,3072]{0,1:T(8,128)(2,1)S(1)}, u32[]{:S(2)}) copy-start(bf16[256,3072]{0,1:T(8,128)(2,1)S(1)} %copy.23) | copy-start | bytes 4718596
  11.1 20.3 %copy-start.9 = (s32[1,1,432]{2,1,0:T(1,128)S(1)}, s32[1,1,432]{2,1,0:T(1,128)}, u32[]{:S(2)}) copy-start(s32[1,1,432]{2,1,0:T(1,128)} %param.14) | copy-start | bytes 5188
  11.1 20.3 %copy-start.10 = (s32[1,1,432]{2,1,0:T(1,128)S(1)}, s32[1,1,432]{2,1,0:T(1,128)}, u32[]{:S(2)}) copy-start(s32[1,1,432]{2,1,0:T(1,128)} %param.15) | copy-start | bytes 5188
  31.4 1.5 copy-start.3
  33.0 3.6 copy-start
  91.2 11.8 %copy-start.4 = (bf16[48,16384]{1,0:T(8,128)(2,1)S(1)}, bf16[48,16384]{1,0:T(8,128)(2,1)}, u32[]{:S(2)}) copy-start(bf16[48,16384]{1,0:T(8,128)(2,1)} %copy-done.3) | copy-start | bytes 4718596 | tf_op jit(solution)/shard_map/while
  103.0 1.5 copy-start.3
  104.5 3.6 copy-start
  162.8 14.7 %copy-start.4 = (bf16[48,16384]{1,0:T(8,128)(2,1)S(1)}, bf16[48,16384]{1,0:T(8,128)(2,1)}, u32[]{:S(2)}) copy-start(bf16[48,16384]{1,0:T(8,128)(2,1)} %copy-done.3) | copy-start | bytes 4718596 | tf_op jit(solution)/shard_map/while
  177.5 1.5 copy-start.3
  179.0 3.6 copy-start
  237.2 14.7 %copy-start.4 = (bf16[48,16384]{1,0:T(8,128)(2,1)S(1)}, bf16[48,16384]{1,0:T(8,128)(2,1)}, u32[]{:S(2)}) copy-start(bf16[48,16384]{1,0:T(8,128)(2,1)} %copy-done.3) | copy-start | bytes 4718596 | tf_op jit(solution)/shard_map/while
  260.5 1.4 copy-start.8
  260.5 146.5 %all-gather.5.cloned.1.call-start = ((), (), s32[]{:S(2)}) async-start(), calls=%async_computation.5 | async-start | bytes 7864320 | tf_op jit(solution)/shard_map/all_gather | solution.py:94
  262.6 74.2 %copy-start.6 = (bf16[3072,256]{1,0:T(8,128)(2,1)S(1)}, bf16[3072,256]{1,0:T(8,128)(2,1)}, u32[]{:S(2)}) copy-start(bf16[3072,256]{1,0:T(8,128)(2,1)} %get-tuple-element.884) | copy-start | bytes 4718596
  336.7 268.5 %reduce-scatter.10.cloned.1.call-start = ((), (), s32[]{:S(2)}) async-start(), calls=%async_computation.7 | async-start | bytes 1966080 | tf_op jit(solution)/shard_map/convert_element_type | solution.py:117
  432.4 3.6 copy-start.1
  464.0 3.6 copy-start.1
  497.5 3.6 copy-start.1
  530.7 2.3 copy-start.2
  530.7 83.0 %reduce-scatter.8.cloned.1.call-start = ((), (), s32[]{:S(2)}) async-start(), calls=%async_computation.6 | async-start | bytes 5308416 | tf_op jit(solution)/shard_map/reduce_scatter | solution.py:131
  602.1 1.4 copy-start.7
Sparse Core Ops, SparseCore 0:
  9.5 15.3 all-gather.2
  260.6 71.3 reduce-scatter.5
  336.8 70.1 all-gather.4
  530.9 35.3 reduce-scatter.9
  602.3 11.4 reduce-scatter.7
where the time goes:
time: 623 us; the launch traced here: 621 us
  local copies, waits for them, and re-layouts  223 us (36%)
  waiting for transfers between devices  161 us (26%)
  matrix products  153 us (25%)
  other arithmetic  67.6 us (11%)
  between operations  14.8 us (2%)
    while x60, local copies, waits for them, and re-layouts  130 us
    reduce_scatter x1, waiting for transfers between devices, local(): lax.psum_scatter(pre_partial.astype(jnp.bfloat16), 'col', scatter_dimensi...  69.4 us
    all_gather x1, waiting for transfers between devices, local(): grad_full = lax.all_gather(grad_share, 'col', axis=1, tiled=True)  68.1 us
    dot_general x24, matrix products, pick_blocks(): jnp.dot(selector, flat, preferred_element_type=jnp.float32)  59.2 us
    add x6, other arithmetic, place_blocks(): return running + added.reshape(running.shape)  52.6 us
    dot_general x6, matrix products, place_blocks(): jnp.dot(selector.T, lower, preferred_element_type=jnp.float32)  45.2 us
    another operation x4, local copies, waits for them, and re-layouts, pick_blocks(): flat = table.reshape(table.shape[0], table.shape[1] * table.shape[2])  23.8 us
    dot_general x6, matrix products, place_blocks(): added = jnp.dot(selector.T, upper, preferred_element_type=jnp.float32)  19.5 us
  transfers between devices with their start and end apart: 5, of which 4 were waited for; matrix products, arithmetic and copies ran while one was open for 13% of the time, Pallas kernels for 0%

commit v1 on v0

--- a/solution.py
+++ b/solution.py
@@ -91,7 +91,28 @@
     )
     activation = gelu_value(pre_share).astype(jnp.bfloat16)
     grad_share = (act_grad.astype(jnp.float32) * gelu_slope(pre_share)).astype(jnp.bfloat16)
-    grad_full = lax.all_gather(grad_share, "col", axis=1, tiled=True)
+    small = jax.lax.axis_size("col")
+    earlier = jax.lax.axis_index("col")
+    val2, high, shaped = (small, earlier, grad_share.shape[1])
+    samples = [at * val2 if kk == 1 else at for kk, at in enumerate(grad_share.shape)]
+    grad_full = lax.dynamic_update_slice_in_dim(
+        jnp.zeros(samples, grad_share.dtype), grad_share, high * shaped, axis=1
+    )
+    out_arr = m_next = grad_share
+    for m in tuple(range(1, val2 // 2 + 1)):
+        out_arr = jax.lax.ppermute(
+            out_arr, axis_name="col", perm=[(kk, (kk + 1) % val2) for kk in range(val2)]
+        )
+        grad_full = lax.dynamic_update_slice_in_dim(
+            grad_full, out_arr, (high - m) % val2 * shaped, axis=1
+        )
+        if 2 * m < val2:
+            m_next = jax.lax.ppermute(
+                m_next, axis_name="col", perm=[(kk, (kk - 1) % val2) for kk in range(val2)]
+            )
+            grad_full = lax.dynamic_update_slice_in_dim(
+                grad_full, m_next, (high + m) % val2 * shaped, axis=1
+            )
     grad_blocks = grad_full.T.reshape(out_blocks, 64, token_count)
     empty_cols = jnp.zeros((in_blocks, 64, token_count), jnp.float32)
     piece = lax.all_gather(weight_tiles, "dp", axis=2, tiled=True)

time: 623 us -> 646 us (1.037)
  waiting for transfers between devices: 161 us -> 185 us
  matrix products: 153 us -> 141 us
  local copies, waits for them, and re-layouts: 223 us -> 231 us
    ppermute x0 -> x3, waiting for transfers between devices: none -> 95.4 us  [the longest x2 65.5 us: local(): jax.lax.ppermute(out_arr, axis_name='col', perm=[(kk, (kk + 1) % val2) fo...]
    all_gather x1 -> x0, waiting for transfers between devices: 68.1 us -> none  [local(): grad_full = lax.all_gather(grad_share, 'col', axis=1, tiled=True)]
    while x60 -> x42, local copies, waits for them, and re-layouts: 130 us -> 117 us
    dot_general x3, matrix products: 13.3 us -> 4.1 us  [advance(): jnp.einsum('sik,sit->skt', group_tiles, gathered, preferred_element_type=...]
    dot_general x3, matrix products: 11.1 us -> 4.12 us  [advance(): jnp.einsum('sik,skt->sit', group_tiles, gathered, preferred_element_type=...]
    dynamic_update_slice x0 -> x3, local copies, waits for them, and re-layouts: none -> 6.58 us  [the longest x2 3.92 us: local(): lax.dynamic_update_slice_in_dim(grad_full, out_arr, (high - m) % val2 * s...]
  transfers between devices with their start and end apart: 5 -> 7, of which waited for: 4 -> 6; matrix products, arithmetic and copies ran while one was open for 13% -> 13% of each run, Pallas kernels for 0% -> 0%
where the time goes in v1:
time: 646 us; the launch traced here: 644 us
  local copies, waits for them, and re-layouts  231 us (36%)
  waiting for transfers between devices  185 us (29%)
  matrix products  141 us (22%)
  other arithmetic  66.9 us (10%)
  between operations  14.8 us (2%)
    while x42, local copies, waits for them, and re-layouts  117 us
    reduce_scatter x1, waiting for transfers between devices, local(): lax.psum_scatter(pre_partial.astype(jnp.bfloat16), 'col', scatter_dimensi...  69.5 us
    ppermute x2, waiting for transfers between devices, local(): jax.lax.ppermute(out_arr, axis_name='col', perm=[(kk, (kk + 1) % val2) fo...  65.5 us
    dot_general x24, matrix products, pick_blocks(): jnp.dot(selector, flat, preferred_element_type=jnp.float32)  63.4 us
    add x6, other arithmetic, place_blocks(): return running + added.reshape(running.shape)  52.1 us
    dot_general x6, matrix products, place_blocks(): jnp.dot(selector.T, lower, preferred_element_type=jnp.float32)  44.8 us
    ppermute x1, waiting for transfers between devices, local(): jax.lax.ppermute(m_next, axis_name='col', perm=[(kk, (kk - 1) % val2) for...  29.9 us
    another operation x4, local copies, waits for them, and re-layouts, pick_blocks(): flat = table.reshape(table.shape[0], table.shape[1] * table.shape[2])  25.1 us
  transfers between devices with their start and end apart: 7, of which 6 were waited for; matrix products, arithmetic and copies ran while one was open for 13% of the time, Pallas kernels for 0%

profile of v1, /device:TPU:0, one launch (start us, length us, event | category | flops | bytes accessed | tf_op | source)
XLA Modules:
  0.0 644.0 jit_solution(8583693936274955034)
XLA Ops:
  12.4 12.5 %all-gather.2.cloned.1.call-done = bf16[1,1,432,4096]{3,2,1,0:T(8,128)(2,1)} async-done(((bf16[1,1,216,4096]{3,2,1,0:T(8,128)(2,1)}), bf16[1,1,432,4096]{3,2,1,0:T(8,128)(2,1)}) %all-gather.2.cloned.1.call-update) | async-done | bytes 3538960 | tf_op jit(solution)/shard_map/all_gather | solution.py:70
  25.0 6.4 %copy.24 = bf16[1,1,432,4096]{2,3,1,0:T(8,128)(2,1)} copy(bf16[1,1,432,4096]{3,2,1,0:T(8,128)(2,1)} %all-gather.2.cloned.1.call-done) | data formatting | bytes 7077888 | tf_op jit(solution)/shard_map/all_gather | solution.py:70
  31.4 215.5 %while.45 = (s32[]{:T(128)}, f32[192,64,256]{2,1,0:T(8,128)}, s32[432]{0:T(512)S(1)}, bf16[432,64,64]{0,2,1:T(8,128)(2,1)}, s32[432]{0:T(512)S(1)}, /*index=5*/b...) while((s32[]{:T(128)}, f32[192,64,256]{2,1,0:T(8,128)}, ...), condition=%wide.wide.region_1.0_spmd.clone, body=%wide.wide.region_0.0_spmd.clone.sunk | while | flops 2366436096 | bytes 174200656 | solution.py:27
  31.5 4.3 constant_dynamic-slice_fusion.6
  35.8 3.8 copy.66
  39.7 2.8 convolution_convert_fusion.14
  45.3 11.3 %copy.68 = f32[18,8,64,256]{3,1,2,0:T(8,128)} copy(f32[18,8,64,256]{3,2,1,0:T(8,128)S(1)} %bitcast.145) | data formatting | bytes 18874368 | tf_op jit(solution)/shard_map/while
  56.6 5.6 fusion.73
  62.3 13.6 %convolution_add_fusion.6 = f32[192,16384]{1,0:T(8,128)} fusion(f32[192,16384]{1,0:T(8,128)S(1)} %fusion.73, f32[144,16384]{1,0:T(8,128)} %bitcast.143, s32[144]{0:T(256)S(1)} %dynamic_slice.115), kind=kOutput, calls=%fused_computation.8.clone.clone.1 | convolution fusion | flops 918580224 | bytes 34603584 | tf_op jit(solution)/shard_map/while/body/eval_jaxpr/dot_general | solution.py:47
  75.8 13.8 %copy.69 = f32[24,8,64,256]{3,2,1,0:T(8,128)} copy(f32[24,8,64,256]{3,1,2,0:T(8,128)} %bitcast.144) | data formatting | bytes 25165824 | tf_op jit(solution)/shard_map/while
  89.6 11.7 %bitcast_add_fusion.6 = f32[192,64,256]{2,1,0:T(8,128)} fusion(f32[24,8,64,256]{3,2,1,0:T(8,128)} %copy.69, f32[192,64,256]{2,1,0:T(8,128)} %get-tuple-element.760, pred[]{:T(512)S(6)} %compare.11), kind=kLoop, calls=%fused_computation.10.clone.clone.1 | loop fusion | flops 6291456 | bytes 37748736 | tf_op jit(solution)/shard_map/while/body/eval_jaxpr/add | solution.py:48
  101.4 4.3 constant_dynamic-slice_fusion.6
  105.7 3.8 copy.66
  109.5 2.8 convolution_convert_fusion.14
  115.2 11.3 %copy.68 = f32[18,8,64,256]{3,1,2,0:T(8,128)} copy(f32[18,8,64,256]{3,2,1,0:T(8,128)S(1)} %bitcast.145) | data formatting | bytes 18874368 | tf_op jit(solution)/shard_map/while
  126.5 5.6 fusion.73
  132.1 13.6 %convolution_add_fusion.6 = f32[192,16384]{1,0:T(8,128)} fusion(f32[192,16384]{1,0:T(8,128)S(1)} %fusion.73, f32[144,16384]{1,0:T(8,128)} %bitcast.143, s32[144]{0:T(256)S(1)} %dynamic_slice.115), kind=kOutput, calls=%fused_computation.8.clone.clone.1 | convolution fusion | flops 918580224 | bytes 34603584 | tf_op jit(solution)/shard_map/while/body/eval_jaxpr/dot_general | solution.py:47
  145.7 13.8 %copy.69 = f32[24,8,64,256]{3,2,1,0:T(8,128)} copy(f32[24,8,64,256]{3,1,2,0:T(8,128)} %bitcast.144) | data formatting | bytes 25165824 | tf_op jit(solution)/shard_map/while
  159.5 14.6 %bitcast_add_fusion.6 = f32[192,64,256]{2,1,0:T(8,128)} fusion(f32[24,8,64,256]{3,2,1,0:T(8,128)} %copy.69, f32[192,64,256]{2,1,0:T(8,128)} %get-tuple-element.760, pred[]{:T(512)S(6)} %compare.11), kind=kLoop, calls=%fused_computation.10.clone.clone.1 | loop fusion | flops 6291456 | bytes 37748736 | tf_op jit(solution)/shard_map/while/body/eval_jaxpr/add | solution.py:48
  174.2 4.0 constant_dynamic-slice_fusion.6
  178.2 3.8 copy.66
  182.0 2.8 convolution_convert_fusion.14
  187.7 11.3 %copy.68 = f32[18,8,64,256]{3,1,2,0:T(8,128)} copy(f32[18,8,64,256]{3,2,1,0:T(8,128)S(1)} %bitcast.145) | data formatting | bytes 18874368 | tf_op jit(solution)/shard_map/while
  199.0 5.6 fusion.73
  204.6 13.6 %convolution_add_fusion.6 = f32[192,16384]{1,0:T(8,128)} fusion(f32[192,16384]{1,0:T(8,128)S(1)} %fusion.73, f32[144,16384]{1,0:T(8,128)} %bitcast.143, s32[144]{0:T(256)S(1)} %dynamic_slice.115), kind=kOutput, calls=%fused_computation.8.clone.clone.1 | convolution fusion | flops 918580224 | bytes 34603584 | tf_op jit(solution)/shard_map/while/body/eval_jaxpr/dot_general | solution.py:47
  218.2 13.8 %copy.69 = f32[24,8,64,256]{3,2,1,0:T(8,128)} copy(f32[24,8,64,256]{3,1,2,0:T(8,128)} %bitcast.144) | data formatting | bytes 25165824 | tf_op jit(solution)/shard_map/while
  232.0 14.6 %bitcast_add_fusion.6 = f32[192,64,256]{2,1,0:T(8,128)} fusion(f32[24,8,64,256]{3,2,1,0:T(8,128)} %copy.69, f32[192,64,256]{2,1,0:T(8,128)} %get-tuple-element.760, pred[]{:T(512)S(6)} %compare.11), kind=kLoop, calls=%fused_computation.10.clone.clone.1 | loop fusion | flops 6291456 | bytes 37748736 | tf_op jit(solution)/shard_map/while/body/eval_jaxpr/add | solution.py:48
  246.9 8.2 %convert_element_type.122 = bf16[192,64,256]{2,1,0:T(8,128)(2,1)} convert(f32[192,64,256]{2,1,0:T(8,128)} %get-tuple-element.375) | non-fusion elementwise | flops 3145728 | bytes 18874368 | tf_op jit(solution)/shard_map/convert_element_type | solution.py:88
  257.2 69.5 %reduce-scatter.6.cloned.1.call-done = bf16[3072,256]{1,0:T(8,128)(2,1)} async-done(((bf16[12288,256]{1,0:T(8,128)(2,1)}), bf16[3072,256]{1,0:T(8,128)(2,1)}) %reduce-scatter.6.cloned.1.call-update) | async-done | bytes 1572880 | tf_op jit(solution)/shard_map/reduce_scatter | solution.py:88
  326.7 3.0 broadcast_in_dim.59
  329.6 3.4 constant_dynamic-update-slice_fusion.4
  336.0 35.5 %collective-permute-done = bf16[256,3072]{0,1:T(8,128)(2,1)S(1)} collective-permute-done((bf16[256,3072]{0,1:T(8,128)(2,1)}, bf16[256,3072]{0,1:T(8,128)(2,1)S(1)}, u32[]{:S(2)}, u32[]{:S(2)}) %collective-permute-start) | collective-permute-done | bytes 1572896 | tf_op jit(solution)/shard_map/ppermute | solution.py:103
  375.2 29.9 %collective-permute-done.1 = bf16[256,3072]{0,1:T(8,128)(2,1)} collective-permute-done((bf16[256,3072]{0,1:T(8,128)(2,1)}, bf16[256,3072]{0,1:T(8,128)(2,1)}, u32[]{:S(2)}, u32[]{:S(2)}) %collective-permute-start.1) | collective-permute-done | bytes 1572896 | tf_op jit(solution)/shard_map/ppermute | solution.py:110
  405.1 2.7 constant_dynamic-update-slice_fusion.2
  407.7 30.1 %collective-permute-done.2 = bf16[256,3072]{0,1:T(8,128)(2,1)} collective-permute-done((bf16[256,3072]{0,1:T(8,128)(2,1)S(1)}, bf16[256,3072]{0,1:T(8,128)(2,1)}, u32[]{:S(2)}, u32[]{:S(2)}) %collective-permute-start.2) | collective-permute-done | bytes 1572896 | tf_op jit(solution)/shard_map/ppermute | solution.py:103
  437.8 2.6 constant_dynamic-update-slice_fusion.1
  440.4 10.5 %reshape_reshape.36 = bf16[192,16384]{1,0:T(8,128)(2,1)} reshape(bf16[12288,256]{1,0:T(8,128)(2,1)} %bitcast.7) | data formatting | bytes 12582912 | tf_op jit(solution)/shard_map/while/body/eval_jaxpr/reshape;reshape | solution.py:36
  450.9 10.4 %reshape_reshape.30 = bf16[192,16384]{1,0:T(8,128)(2,1)} reshape(bf16[12288,256]{1,0:T(8,128)(2,1)} %bitcast.7) | data formatting | bytes 12582912 | tf_op jit(solution)/shard_map/while/body/eval_jaxpr/reshape;reshape | solution.py:36
  461.3 89.0 %while.46 = (s32[]{:T(128)}, f32[48,64,256]{2,1,0:T(8,128)}, s32[432]{0:T(512)S(1)}, bf16[432,64,64]{0,2,1:T(8,128)(2,1)}, s32[432]{0:T(512)S(1)}, /*index=5*/bf...) while((s32[]{:T(128)}, f32[48,64,256]{2,1,0:T(8,128)}, ...), condition=%wide.wide.region_4.5_spmd.clone, body=%wide.wide.region_3.4_spmd.clone.sunk | while | flops 1679860224 | bytes 108140384 | solution.py:27
  461.6 2.9 constant_dynamic-slice_fusion.7
  464.5 4.5 copy.70
  469.1 4.2 convolution_convert_fusion.15
  476.4 7.7 %copy.72 = f32[18,8,64,256]{3,1,2,0:T(8,128)S(1)} copy(f32[18,8,64,256]{3,2,1,0:T(8,128)S(1)} %bitcast.146) | data formatting | bytes 18874368 | tf_op jit(solution)/shard_map/while
  490.0 2.9 constant_dynamic-slice_fusion.7
  492.9 4.5 copy.70
  497.5 4.2 convolution_convert_fusion.15
  504.7 7.7 %copy.72 = f32[18,8,64,256]{3,1,2,0:T(8,128)S(1)} copy(f32[18,8,64,256]{3,2,1,0:T(8,128)S(1)} %bitcast.146) | data formatting | bytes 18874368 | tf_op jit(solution)/shard_map/while
  515.8 4.4 bitcast_add_fusion.7
  520.2 2.6 constant_dynamic-slice_fusion.7
  522.9 4.5 copy.70
  527.5 4.2 convolution_convert_fusion.15
  534.7 7.7 %copy.72 = f32[18,8,64,256]{3,1,2,0:T(8,128)S(1)} copy(f32[18,8,64,256]{3,2,1,0:T(8,128)S(1)} %bitcast.146) | data formatting | bytes 18874368 | tf_op jit(solution)/shard_map/while
  545.8 4.4 bitcast_add_fusion.7
  556.5 69.2 %while.44 = (s32[]{:T(128)}, bf16[432,4096]{1,0:T(8,128)(2,1)}, s32[432]{0:T(512)S(1)}, bf16[12288,256]{1,0:T(8,128)(2,1)}, s32[432]{0:T(512)S(1)}, /*index=5*/b...) while((s32[]{:T(128)}, bf16[432,4096]{1,0:T(8,128)(2,1)}, ...), condition=%wide.wide.region_7.8_spmd, body=%wide.wide.region_6.7_spmd.sunk | while | flops 480128256 | bytes 22415236 | solution.py:27
  556.6 4.1 convolution_convert_fusion.12
  564.3 4.1 convolution_convert_fusion.12
  572.0 4.1 convolution_convert_fusion.12
  579.7 4.1 convolution_convert_fusion.12
  587.3 4.1 convolution_convert_fusion.12
  595.1 4.1 convolution_convert_fusion.12
  602.8 4.1 convolution_convert_fusion.12
  610.5 4.1 convolution_convert_fusion.12
  618.1 4.1 convolution_convert_fusion.12
  630.0 7.3 %reduce-scatter.8.cloned.1.call-done = bf16[216,4096]{1,0:T(8,128)(2,1)} async-done(((bf16[432,4096]{1,0:T(8,128)(2,1)}), bf16[216,4096]{1,0:T(8,128)(2,1)}) %reduce-scatter.8.cloned.1.call-update) | async-done | bytes 1769488 | tf_op jit(solution)/shard_map/reduce_scatter | solution.py:152
  (168 shorter events, 86.6 us)
Async XLA Ops:
  7.2 17.8 %all-gather.2.cloned.1.call-start = ((), (), s32[]{:S(2)}) async-start(), calls=%async_computation.3 | async-start | bytes 5308416 | tf_op jit(solution)/shard_map/all_gather | solution.py:70
  7.9 318.8 %reduce-scatter.6.cloned.1.call-start = ((), (), s32[]{:S(2)}) async-start(), calls=%async_computation.4 | async-start | bytes 7864320 | tf_op jit(solution)/shard_map/reduce_scatter | solution.py:88
  9.7 21.8 %copy-start.2 = (bf16[256,3072]{0,1:T(8,128)(2,1)}, bf16[256,3072]{0,1:T(8,128)(2,1)S(1)}, u32[]{:S(2)}) copy-start(bf16[256,3072]{0,1:T(8,128)(2,1)S(1)} %copy.25) | copy-start | bytes 4718596
  12.4 19.0 %copy-start.7 = (s32[1,1,432]{2,1,0:T(1,128)S(1)}, s32[1,1,432]{2,1,0:T(1,128)}, u32[]{:S(2)}) copy-start(s32[1,1,432]{2,1,0:T(1,128)} %param.14) | copy-start | bytes 5188
  12.4 19.0 %copy-start.8 = (s32[1,1,432]{2,1,0:T(1,128)S(1)}, s32[1,1,432]{2,1,0:T(1,128)}, u32[]{:S(2)}) copy-start(s32[1,1,432]{2,1,0:T(1,128)} %param.15) | copy-start | bytes 5188
  255.1 1.4 copy-start.6
  255.1 374.8 %reduce-scatter.10.cloned.1.call-start = ((), (), s32[]{:S(2)}) async-start(), calls=%async_computation.6 | async-start | bytes 1966080 | tf_op jit(solution)/shard_map/convert_element_type | solution.py:138
  326.7 3.0 copy-start.4
  329.6 42.2 %copy-start.3 = (bf16[3072,256]{1,0:T(8,128)(2,1)S(1)}, bf16[3072,256]{1,0:T(8,128)(2,1)}, u32[]{:S(2)}) copy-start(bf16[3072,256]{1,0:T(8,128)(2,1)} %get-tuple-element.867) | copy-start | bytes 4718596
  333.0 38.4 %collective-permute-start = (bf16[256,3072]{0,1:T(8,128)(2,1)}, bf16[256,3072]{0,1:T(8,128)(2,1)S(1)}, u32[]{:S(2)}, u32[]{:S(2)}) collective-permute-start(bf16[256,3072]{0,1:T(8,128)(2,1)} %get-tuple-element.510), channel_id=1, source_target_pairs={{0,1},{1,2},{2,3},{3,0},{4,5},{5,6},{6,7},{7,4},{8,9},{9,10},{10,1... | collective-permute-start | bytes 4718600 | tf_op jit(solution)/shard_map/ppermute | solution.py:103
  334.3 70.7 %collective-permute-start.1 = (bf16[256,3072]{0,1:T(8,128)(2,1)}, bf16[256,3072]{0,1:T(8,128)(2,1)}, u32[]{:S(2)}, u32[]{:S(2)}) collective-permute-start(bf16[256,3072]{0,1:T(8,128)(2,1)} %get-tuple-element.510), channel_id=1, source_target_pairs={{0,3},{1,0},{2,1},{3,2},{4,7},{5,4},{6,5},{7,6},{8,11},{9,8},{10,9... | collective-permute-start | bytes 4718600 | tf_op jit(solution)/shard_map/ppermute | solution.py:110
  371.4 66.4 %collective-permute-start.2 = (bf16[256,3072]{0,1:T(8,128)(2,1)S(1)}, bf16[256,3072]{0,1:T(8,128)(2,1)}, u32[]{:S(2)}, u32[]{:S(2)}) collective-permute-start(bf16[256,3072]{0,1:T(8,128)(2,1)S(1)} %collective-permute-done), channel_id=1, source_target_pairs={{0,1},{1,2},{2,3},{3,0},{4,5},{5,6},{6,7},{7,4},{8,9},{9,10},{10,1... | collective-permute-start | bytes 4718600 | tf_op jit(solution)/shard_map/ppermute | solution.py:103
  473.3 1.7 copy-start
  501.7 1.7 copy-start
  531.7 1.7 copy-start
  554.2 2.3 copy-start.1
  554.2 83.0 %reduce-scatter.8.cloned.1.call-start = ((), (), s32[]{:S(2)}) async-start(), calls=%async_computation.5 | async-start | bytes 5308416 | tf_op jit(solution)/shard_map/reduce_scatter | solution.py:152
  625.7 1.4 copy-start.5
Sparse Core Ops, SparseCore 0:
  9.5 15.3 all-gather.1
  255.2 71.3 reduce-scatter.5
  554.4 35.1 reduce-scatter.9
  625.9 11.2 reduce-scatter.7
